TPU v7x, 32 devices: a whole 2x2x4 slice. The times are simulated.
32 devices in a mesh: tile: 16 (over z, y, core), inner: 2 (over x).
Axes of the slice: x: 2, y: 2, z: 4, core: 2. Of those that a mesh axis runs over, the one named last changes fastest.
Arguments:
- amplitudes: bfloat16 [512, 4096], P('tile', 'inner'), may hold values from -6 to 6
- left_factors: bfloat16 [1024, 4096], P('tile', 'inner'), may hold values from -0.1875 to 0.1875
- right_factors: bfloat16 [1024, 16384], P(None, 'tile'), may hold values from -0.1875 to 0.1875
- tile_pattern: int32 [8, 32], replicated, may hold values from 0 to 1, as said below
- occupied_shift: float32 [512], P('inner'), may hold values from 0.5 to 2
- virtual_shift: float32 [16384], P('tile'), may hold values from 0.5 to 5
Outputs:
- residual: float32 [512, 16384], P('inner', 'tile')
Inputs may be any that keep to these rules, and one draw needn't show every extreme that they name: `tile_pattern`: 1 where the tiles interact, 0 where their integrals are dropped.
All inputs are finite; a program needn't handle non-finite values.
Results may differ from a plain program's by a relative error of at most 0.0029.
Values may be sent and summed in bfloat16 or wider, within the bound.
No kernel may reach another device: no remote copies, remote signals or barrier semaphores. Data moves between devices by JAX's collectives and lax.ppermute only.
A program may use at most 64 MiB of HBM per device.

v0:
```python
import functools

import jax
import jax.numpy as jnp
from jax import lax
from jax.experimental import pallas as pl
from jax.experimental.pallas import tpu as pltpu
from jax.sharding import PartitionSpec as P


TILE = 512
VMEM = pl.BlockSpec(memory_space=pltpu.VMEM)
SMEM = pl.BlockSpec(memory_space=pltpu.SMEM)
ANY = pl.BlockSpec(memory_space=pl.ANY)
PARAMS = pltpu.CompilerParams(vmem_limit_bytes=20 * 1024 * 1024)


def cost(flops, moved):
    return pl.CostEstimate(flops=int(flops), bytes_accessed=int(moved), transcendentals=0)


def keep_kernel(amplitudes, left, kept):
    rows = amplitudes.shape[0]
    kept[:rows, :] = amplitudes[...]
    kept[rows:, :] = left[...]


def place():
    t = lax.axis_index("tile")
    return t // 4, lax.rem(t // 2, 2), lax.rem(t, 2), lax.axis_index("inner")


def multiply(parts, a_refs, l_all, outs, a_all, result):
    z, _, _, inner = place()
    rows, width = a_refs[0].shape
    for r, ref in enumerate(a_refs):
        a_all[r * rows : (r + 1) * rows, :] = ref[...].astype(a_all.dtype)
    for c in range(width // TILE):
        cols = slice(c * TILE, (c + 1) * TILE)
        result[...] = lax.dot_general(
            a_all[:, cols].astype(jnp.bfloat16),
            l_all[:, cols],
            (((1,), (1,)), ((), ())),
            preferred_element_type=jnp.float32,
        )
        for p in range(len(outs) // 2):
            start = pl.multiple_of((inner ^ p ^ (z // parts)) * rows, rows)
            value = result[pl.ds(start, rows), :]
            outs[2 * p][c] = value
            outs[2 * p + 1][c] = value.astype(jnp.bfloat16)


def first_products_kernel(inner_size, parts, kept, *refs):
    a_refs, l_refs = refs[: inner_size - 1], refs[inner_size - 1 : inner_size + 2]
    outs = refs[inner_size + 2 : 3 * inner_size + 2]
    l_all, a_all, result = refs[3 * inner_size + 2 :]
    _, y, core, _ = place()
    block = l_refs[0].shape[0]
    rows = kept.shape[0] - block
    for q, ref in enumerate((kept.at[rows:, :],) + l_refs):
        where = ((y ^ (q // 2)) * 2 + (core ^ (q % 2))) * block
        l_all[pl.ds(pl.multiple_of(where, block), block), :] = ref[...]
    multiply(parts, (kept.at[:rows, :],) + a_refs, l_all, outs, a_all, result)


def next_products_kernel(inner_size, parts, *refs):
    a_refs, l_all = refs[:inner_size], refs[inner_size]
    outs = refs[inner_size + 1 : 3 * inner_size + 1]
    a_all, result = refs[3 * inner_size + 1 :]
    multiply(parts, a_refs, l_all, outs, a_all, result)


def weights_kernel(inner_size, left_tiles, right_tiles, targets, rows, mask, out):
    z, y, core, inner = place()
    chip = z * 2 + y
    count = inner_size * left_tiles
    lanes = mask.shape[2]
    lane = lax.broadcasted_iota(jnp.int32, (rows, count * rows), 1)
    diagonal = lax.rem(lane, rows) == lax.broadcasted_iota(jnp.int32, (rows, count * rows), 0)
    block = lane // rows
    for m in range(targets):
        for d in range(right_tiles):
            column = ((chip ^ m) * 2 + core) * right_tiles + d
            value = jnp.zeros((rows, count * rows), jnp.float32)
            for i in range(count):
                row = (inner ^ (i // left_tiles)) * left_tiles + i % left_tiles
                on = mask[row, pl.ds(column, 1), :]
                value = jnp.where(block == i, jnp.concatenate([on] * (count * rows // lanes), axis=1), value)
            at = (m * right_tiles + d) * rows
            out[at : at + rows, :] = jnp.where(diagonal, value, 0.0).astype(jnp.bfloat16)


def totals_kernel(inner_size, right_tiles, weights, *refs):
    count = 4 * inner_size
    sources, outs = refs[:count], refs[count:]
    left_tiles, rows, depth = sources[0].shape
    shape = (left_tiles * rows, depth)
    for b in range(2):
        for rel in range(2):
            high, low = [], []
            for p in range(inner_size):
                ref = sources[(b * 2 + rel) * inner_size + p]
                value = ref[...]
                if ref.dtype == jnp.float32 or rows % 16:
                    value = value.astype(jnp.float32).reshape(shape)
                    rounded = value.astype(jnp.bfloat16)
                    low.append((value - rounded.astype(jnp.float32)).astype(jnp.bfloat16))
                    value = rounded
                high.append(value.reshape(shape))
            total = jnp.dot(weights[...], jnp.concatenate(high, axis=0), preferred_element_type=jnp.float32)
            if b == 0:
                total += jnp.dot(weights[...], jnp.concatenate(low, axis=0), preferred_element_type=jnp.float32)
            for m, out in enumerate(outs):
                for d in range(right_tiles):
                    at = (m * right_tiles + d) * rows
                    out[d, b, rel * rows : (rel + 1) * rows, :] = total[at : at + rows, :].astype(jnp.bfloat16)


def inverse_kernel(occupied, virtual, out):
    lanes = 128
    column = jnp.broadcast_to(occupied[...], (lanes, out.shape[0])).T
    for at in range(0, out.shape[1], lanes):
        out[:, at : at + lanes] = 1.0 / (column + virtual[:, at : at + lanes])


def gather_kernel(parts, part, last, z_half, *refs):
    targets = 4 * z_half // 2
    t_refs, right, rest = refs[:targets], refs[targets], refs[targets + 1 :]
    so_far, rest = (rest[0], rest[1:]) if part else (None, rest)
    if last:
        inverse, out, staged, sem = rest
    else:
        (out,) = rest
    z, y, core, _ = place()
    right_tiles, _, both, depth = t_refs[0].shape
    low, rows = lax.rem(z, parts), both // 2
    for d in range(right_tiles):
        cols = slice(d * TILE, (d + 1) * TILE)
        for o in range(parts):
            here = slice(o * 2 * both, (o + 1) * 2 * both)
            total = None if so_far is None else so_far[here, cols]
            for q in range(targets // 2):
                if q % parts != o ^ part:
                    continue
                for b in range(2):
                    left = jnp.concatenate([t_refs[2 * q][d, b], t_refs[2 * q + 1][d, b]], axis=0)
                    at = pl.ds(pl.multiple_of((z ^ q ^ (b * z_half)) * depth, depth), depth)
                    term = jnp.dot(left, right[at, cols], preferred_element_type=jnp.float32)
                    total = term if total is None else total + term
            if not last:
                out[here, cols] = total
                continue
            for i in range(4):
                at = (((low ^ o) * 2 + (y ^ (i // 2))) * 2 + (core ^ (i % 2))) * rows
                at = pl.ds(pl.multiple_of(at, rows), rows)
                staged[at, cols] = total[i * rows : (i + 1) * rows, :] * inverse[at, cols]
        if last:
            pltpu.make_async_copy(staged.at[:, cols], out.at[:, cols], sem.at[d]).start()
    if last:
        for d in range(right_tiles):
            cols = slice(d * TILE, (d + 1) * TILE)
            pltpu.make_async_copy(staged.at[:, cols], out.at[:, cols], sem.at[d]).wait()


def solution(mesh):
    tiles, inner_size = mesh.shape["tile"], mesh.shape["inner"]
    z_size, chips = tiles // 4, tiles // 2
    parts, half, z_half = z_size // inner_size, chips // 2, z_size // 2

    def swap(value, q, axis="tile", size=tiles):
        return lax.ppermute(value, axis, [(t, t ^ q) for t in range(size)])

    def cross(value, p):
        pairs = [
            (t * inner_size + n, (t ^ (4 * z_half)) * inner_size + (n ^ p))
            for t in range(tiles)
            for n in range(inner_size)
        ]
        return lax.ppermute(value, ("tile", "inner"), pairs)

    def call(name, kernel, operands, in_specs, out_shape, scratch=(), flops=0, moved=1 << 20):
        many = isinstance(out_shape, list)
        return pl.pallas_call(
            kernel,
            out_shape=out_shape,
            in_specs=in_specs,
            out_specs=[VMEM] * len(out_shape) if many else ANY if name == "residual" else VMEM,
            scratch_shapes=list(scratch),
            compiler_params=PARAMS,
            cost_estimate=cost(flops, moved),
        )(*operands)

    def on_device(amplitudes, left_factors, right_factors, tile_pattern, occupied_shift, virtual_shift):
        rows, width = amplitudes.shape
        block = left_factors.shape[0]
        out_width = right_factors.shape[1]
        left_tiles, right_tiles = width // TILE, out_width // TILE
        depth = 4 * block

        lanes = min(128, depth)
        on = (tile_pattern != 0).astype(jnp.float32)
        mask = jnp.broadcast_to(on[:, :, None], (*tile_pattern.shape, lanes))
        weights = call(
            "weights",
            functools.partial(weights_kernel, inner_size, left_tiles, right_tiles, half, rows),
            (mask,),
            [VMEM],
            pltpu.VMEM((half * right_tiles * rows, inner_size * left_tiles * rows), jnp.bfloat16),
        )
        kept = call(
            "keep",
            keep_kernel,
            (amplitudes, left_factors),
            [VMEM] * 2,
            pltpu.VMEM((rows + block, width), amplitudes.dtype),
        )
        by_y = swap(left_factors, 2)
        lefts = [swap(left_factors, 1), by_y, swap(by_y, 1)]
        amps = {q: swap(amplitudes, 4 * q) for q in range(1, z_half + 1)}
        amps |= {q: swap(amps[z_half], 4 * (q ^ z_half)) for q in range(z_half + 1, z_size)}

        packed = jnp.bfloat16 if rows % 16 == 0 else jnp.float32
        scratch = [
            pltpu.VMEM((inner_size * rows, width), packed),
            pltpu.VMEM((inner_size * rows, depth), jnp.float32),
        ]
        shapes = [
            pltpu.VMEM((left_tiles, rows, depth), kind)
            for _ in range(inner_size)
            for kind in (jnp.float32, jnp.bfloat16)
        ]
        flops = 2 * inner_size * rows * width * depth
        arrived = []
        for s in range(parts):
            blocks = [amps[r * parts + s] for r in range(inner_size) if r or s]
            if s == 0:
                *products, left_all = call(
                    "products0",
                    functools.partial(first_products_kernel, inner_size, parts),
                    (kept, *blocks, *lefts),
                    [VMEM] * (inner_size + 3),
                    shapes + [pltpu.VMEM((depth, width), jnp.bfloat16)],
                    scratch,
                    flops,
                )
            else:
                products = call(
                    f"products{s}",
                    functools.partial(next_products_kernel, inner_size, parts),
                    (*blocks, left_all),
                    [VMEM] * (inner_size + 1),
                    shapes,
                    scratch,
                    flops,
                )
            crossed = [cross(products[2 * p + 1], p) for p in range(inner_size)]
            mine = [products[0]]
            mine += [swap(products[2 * p], p, "inner", inner_size) for p in range(1, inner_size)]
            other = [swap(part, 1) for part in mine]
            crossed_other = [swap(part, 1) for part in crossed]
            operands = (weights, *mine, *other, *crossed, *crossed_other)
            made = call(
                f"totals{s}",
                functools.partial(totals_kernel, inner_size, right_tiles),
                operands,
                [VMEM] * len(operands),
                [pltpu.VMEM((right_tiles, 2, 2 * rows, depth), jnp.bfloat16)] * half,
            )
            arrived.append([made[0]] + [swap(made[m], 2 * m) for m in range(1, half)])

        result_shape = (occupied_shift.shape[0], out_width)
        inverse = call(
            "inverse",
            inverse_kernel,
            (occupied_shift.reshape(1, -1), virtual_shift.reshape(1, -1)),
            [VMEM] * 2,
            pltpu.VMEM(result_shape, jnp.float32),
        )
        sums = ()
        for s in range(parts):
            last = s == parts - 1
            operands = (*arrived[s], right_factors, *sums) + ((inverse,) if last else ())
            sums = (
                call(
                    "residual" if last else f"sums{s}",
                    functools.partial(gather_kernel, parts, s, last, z_half),
                    operands,
                    [VMEM] * len(operands),
                    jax.ShapeDtypeStruct(result_shape, jnp.float32) if last else pltpu.VMEM(result_shape, jnp.float32),
                    [pltpu.VMEM(result_shape, jnp.float32), pltpu.SemaphoreType.DMA((right_tiles,))] if last else (),
                    2 * occupied_shift.shape[0] * out_width * right_factors.shape[0] // parts,
                    4 << 20,
                ),
            )
        return sums[0]


    placed = (P("tile", "inner"), P("tile", "inner"), P(None, "tile"), P(), P("inner"), P("tile"))
    return jax.shard_map(on_device, mesh=mesh, in_specs=placed, out_specs=P("inner", "tile"), check_vma=False)
```

profile of v0, /device:TPU:0, one launch (start us, length us, event | category | flops | bytes accessed | tf_op | source)
XLA Modules:
  0.0 63.0 jit_solution(8341853507114727662)
XLA Ops:
  0.0 3.0 %collective-permute-start.4 = (bf16[64,2048]{1,0:T(8,128)(2,1)}, bf16[64,2048]{1,0:T(8,128)(2,1)S(1)}, u32[]{:S(2)}, u32[]{:S(2)}) collective-permute-start(bf16[64,2048]{1,0:T(8,128)(2,1)} %left.1), channel_id=1, source_target_pairs={{0,4},{2,6},{4,0},{6,2},{8,12},{10,14},{12,8},{14,10},{16,20},{18,... | collective-permute-start | bytes 786440 | tf_op jit(solution)/shard_map/ppermute | solution.py:171
  3.0 0.0 collective-permute-start.3
  3.0 6.5 %collective-permute-done.4.refs_2_ = bf16[64,2048]{1,0:T(8,128)(2,1)S(1)} collective-permute-done((bf16[64,2048]{1,0:T(8,128)(2,1)}, bf16[64,2048]{1,0:T(8,128)(2,1)S(1)}, u32[]{:S(2)}, u32[]{:S(2)}) %collective-permute-start.4) | collective-permute-done | bytes 262176 | tf_op jit(solution)/shard_map/ppermute | solution.py:171
  9.5 0.0 collective-permute-start.5
  9.5 2.8 %collective-permute-start.1 = (bf16[32,2048]{1,0:T(8,128)(2,1)}, bf16[32,2048]{1,0:T(8,128)(2,1)S(1)}, u32[]{:S(2)}, u32[]{:S(2)}) collective-permute-start(bf16[32,2048]{1,0:T(8,128)(2,1)} %amplitudes.1), channel_id=1, source_target_pairs={{0,16},{2,18},{4,20},{6,22},{8,24},{10,26},{12,28},{14,30},{16,0},... | collective-permute-start | bytes 393224 | tf_op jit(solution)/shard_map/ppermute | solution.py:171
  12.3 1.6 %collective-permute-start = (bf16[32,2048]{1,0:T(8,128)(2,1)}, bf16[32,2048]{1,0:T(8,128)(2,1)S(1)}, u32[]{:S(2)}, u32[]{:S(2)}) collective-permute-start(bf16[32,2048]{1,0:T(8,128)(2,1)} %amplitudes.1), channel_id=1, source_target_pairs={{0,8},{2,10},{4,12},{6,14},{8,0},{10,2},{12,4},{14,6},{16,24},{18,... | collective-permute-start | bytes 393224 | tf_op jit(solution)/shard_map/ppermute | solution.py:171
  13.9 5.7 %collective-permute-done.1.refs_0_ = bf16[32,2048]{1,0:T(8,128)(2,1)S(1)} collective-permute-done((bf16[32,2048]{1,0:T(8,128)(2,1)}, bf16[32,2048]{1,0:T(8,128)(2,1)S(1)}, u32[]{:S(2)}, u32[]{:S(2)}) %collective-permute-start.1) | collective-permute-done | bytes 131104 | tf_op jit(solution)/shard_map/ppermute | solution.py:171
  19.6 0.7 %collective-permute-start.2 = (bf16[32,2048]{1,0:T(8,128)(2,1)S(1)}, bf16[32,2048]{1,0:T(8,128)(2,1)S(1)}, u32[]{:S(2)}, u32[]{:S(2)}) collective-permute-start(bf16[32,2048]{1,0:T(8,128)(2,1)S(1)} %collective-permute-done.1.refs_0_), channel_id=1, source_target_pairs={{0,8},{2,10},{4,12},{6,14},{8,0},{10,2},{12,4},{14,6},{16,24},{18,... | collective-permute-start | bytes 393224 | tf_op jit(solution)/shard_map/ppermute | solution.py:171
  20.3 0.9 %copy-done.1 = bf16[64,2048]{1,0:T(8,128)(2,1)S(1)} copy-done((bf16[64,2048]{1,0:T(8,128)(2,1)S(1)}, bf16[64,2048]{1,0:T(8,128)(2,1)}, u32[]{:S(2)}) %copy-start.1) | copy-done | bytes 262168
  21.3 0.9 %copy-done.2 = bf16[32,2048]{1,0:T(8,128)(2,1)S(1)} copy-done((bf16[32,2048]{1,0:T(8,128)(2,1)S(1)}, bf16[32,2048]{1,0:T(8,128)(2,1)}, u32[]{:S(2)}) %copy-start.2) | copy-done | bytes 131096
  22.2 0.0 collective-permute-done.3.refs_1_
  22.2 0.0 collective-permute-done.5.refs_3_
  22.2 0.6 shard_map.66
  22.8 0.0 copy-start.3
  22.8 0.0 copy-start.4
  22.8 3.3 %collective-permute-start.19 = (bf16[4,32,256]{2,1,0:T(8,128)(2,1)S(1)}, bf16[4,32,256]{2,1,0:T(8,128)(2,1)S(1)}, u32[]{:S(2)}, u32[]{:S(2)}) collective-permute-start(bf16[4,32,256]{2,1,0:T(8,128)(2,1)S(1)} %get-tuple-element.33), channel_id=1, source_target_pairs={{0,16},{1,17},{2,18},{3,19},{4,20},{5,21},{6,22},{7,23},{8,24},{9,... | collective-permute-start | bytes 196616 | tf_op jit(solution)/shard_map/ppermute | solution.py:179
  26.2 1.0 %collective-permute-start.20 = (bf16[4,32,256]{2,1,0:T(8,128)(2,1)S(1)}, bf16[4,32,256]{2,1,0:T(8,128)(2,1)S(1)}, u32[]{:S(2)}, u32[]{:S(2)}) collective-permute-start(bf16[4,32,256]{2,1,0:T(8,128)(2,1)S(1)} %get-tuple-element.34), channel_id=1, source_target_pairs={{0,17},{1,16},{2,19},{3,18},{4,21},{5,20},{6,23},{7,22},{8,25},{9,... | collective-permute-start | bytes 196616 | tf_op jit(solution)/shard_map/ppermute | solution.py:179
  27.2 0.5 collective-permute-start.16
  27.7 1.8 %collective-permute-done.19.refs_4_ = bf16[4,32,256]{2,1,0:T(8,128)(2,1)S(1)} collective-permute-done((bf16[4,32,256]{2,1,0:T(8,128)(2,1)S(1)}, bf16[4,32,256]{2,1,0:T(8,128)(2,1)S(1)}, u32[]{:S(2)}, u32[]{:S(2)}) %collective-permute-start.19) | collective-permute-done | bytes 65568 | tf_op jit(solution)/shard_map/ppermute | solution.py:179
  29.5 0.0 collective-permute-start.21
  29.5 3.8 %collective-permute-done.20.refs_5_ = bf16[4,32,256]{2,1,0:T(8,128)(2,1)S(1)} collective-permute-done((bf16[4,32,256]{2,1,0:T(8,128)(2,1)S(1)}, bf16[4,32,256]{2,1,0:T(8,128)(2,1)S(1)}, u32[]{:S(2)}, u32[]{:S(2)}) %collective-permute-start.20) | collective-permute-done | bytes 65568 | tf_op jit(solution)/shard_map/ppermute | solution.py:179
  33.3 0.0 collective-permute-start.22
  33.3 0.0 collective-permute-done.refs_0_
  33.3 0.0 collective-permute-done.2.refs_1_
  33.4 0.0 copy-start
  33.4 0.5 shard_map.67
  33.8 0.1 collective-permute-start.9
  34.0 3.1 %collective-permute-start.10 = (bf16[4,32,256]{2,1,0:T(8,128)(2,1)S(1)}, bf16[4,32,256]{2,1,0:T(8,128)(2,1)S(1)}, u32[]{:S(2)}, u32[]{:S(2)}) collective-permute-start(bf16[4,32,256]{2,1,0:T(8,128)(2,1)S(1)} %get-tuple-element.26), channel_id=1, source_target_pairs={{0,17},{1,16},{2,19},{3,18},{4,21},{5,20},{6,23},{7,22},{8,25},{9,... | collective-permute-start | bytes 196616 | tf_op jit(solution)/shard_map/ppermute | solution.py:179
  37.0 0.0 collective-permute-done.21.refs_6_
  37.0 1.3 %collective-permute-start.6 = (f32[4,32,256]{2,1,0:T(8,128)S(1)}, f32[4,32,256]{2,1,0:T(8,128)S(1)}, u32[]{:S(2)}, u32[]{:S(2)}) collective-permute-start(f32[4,32,256]{2,1,0:T(8,128)S(1)} %get-tuple-element.24), channel_id=1, source_target_pairs={{0,1},{1,0},{2,3},{3,2},{4,5},{5,4},{6,7},{7,6},{8,9},{9,8},{10,11... | collective-permute-start | bytes 393224 | tf_op jit(solution)/shard_map/ppermute | solution.py:171
  38.3 0.0 collective-permute-done.22.refs_7_
  38.3 0.0 collective-permute-start.17
  38.3 0.0 collective-permute-done.16.refs_1_
  38.3 0.5 collective-permute-start.18
  38.8 5.0 %collective-permute-done.6.refs_1_ = f32[4,32,256]{2,1,0:T(8,128)S(1)} collective-permute-done((f32[4,32,256]{2,1,0:T(8,128)S(1)}, f32[4,32,256]{2,1,0:T(8,128)S(1)}, u32[]{:S(2)}, u32[]{:S(2)}) %collective-permute-start.6) | collective-permute-done | bytes 131104 | tf_op jit(solution)/shard_map/ppermute | solution.py:171
  43.8 0.0 collective-permute-start.7
  43.8 0.0 collective-permute-done.17.refs_2_
  43.8 0.5 collective-permute-start.8
  44.3 0.1 broadcast_in_dim.2.mask
  44.4 0.1 shard_map.64.weights
  44.5 0.0 collective-permute-done.18.refs_3_
  44.5 0.4 shard_map.69
  44.9 1.6 %collective-permute-start.23 = (bf16[2,2,64,256]{3,2,1,0:T(8,128)(2,1)S(1)}, bf16[2,2,64,256]{3,2,1,0:T(8,128)(2,1)S(1)}, u32[]{:S(2)}, u32[]{:S(2)}) collective-permute-start(bf16[2,2,64,256]{3,2,1,0:T(8,128)(2,1)S(1)} %get-tuple-element.36), channel_id=1, source_target_pairs={{0,4},{2,6},{4,0},{6,2},{8,12},{10,14},{12,8},{14,10},{16,20},{18,... | collective-permute-start | bytes 393224 | tf_op jit(solution)/shard_map/ppermute | solution.py:171
  46.5 0.0 collective-permute-done.9.refs_4_
  46.5 0.0 collective-permute-start.11
  46.5 0.0 collective-permute-done.10.refs_5_
  46.5 0.5 collective-permute-start.12
  47.0 0.7 %collective-permute-done.11.refs_6_ = bf16[4,32,256]{2,1,0:T(8,128)(2,1)S(1)} collective-permute-done((bf16[4,32,256]{2,1,0:T(8,128)(2,1)S(1)}, bf16[4,32,256]{2,1,0:T(8,128)(2,1)S(1)}, u32[]{:S(2)}, u32[]{:S(2)}) %collective-permute-start.11) | collective-permute-done | bytes 65568 | tf_op jit(solution)/shard_map/ppermute | solution.py:171
  47.7 0.4 collective-permute-start.24
  48.1 0.0 collective-permute-done.12.refs_7_
  48.1 1.6 %collective-permute-start.25 = (bf16[2,2,64,256]{3,2,1,0:T(8,128)(2,1)S(1)}, bf16[2,2,64,256]{3,2,1,0:T(8,128)(2,1)S(1)}, u32[]{:S(2)}, u32[]{:S(2)}) collective-permute-start(bf16[2,2,64,256]{3,2,1,0:T(8,128)(2,1)S(1)} %get-tuple-element.38), channel_id=1, source_target_pairs={{0,12},{2,14},{4,8},{6,10},{8,4},{10,6},{12,0},{14,2},{16,28},{18,... | collective-permute-start | bytes 393224 | tf_op jit(solution)/shard_map/ppermute | solution.py:171
  49.7 0.4 shard_map.68
  50.1 1.6 %collective-permute-start.13 = (bf16[2,2,64,256]{3,2,1,0:T(8,128)(2,1)S(1)}, bf16[2,2,64,256]{3,2,1,0:T(8,128)(2,1)S(1)}, u32[]{:S(2)}, u32[]{:S(2)}) collective-permute-start(bf16[2,2,64,256]{3,2,1,0:T(8,128)(2,1)S(1)} %get-tuple-element.28), channel_id=1, source_target_pairs={{0,4},{2,6},{4,0},{6,2},{8,12},{10,14},{12,8},{14,10},{16,20},{18,... | collective-permute-start | bytes 393224 | tf_op jit(solution)/shard_map/ppermute | solution.py:171
  51.7 0.4 collective-permute-start.14
  52.0 0.0 collective-permute-done.23.refs_1_
  52.0 1.6 %collective-permute-start.15 = (bf16[2,2,64,256]{3,2,1,0:T(8,128)(2,1)S(1)}, bf16[2,2,64,256]{3,2,1,0:T(8,128)(2,1)S(1)}, u32[]{:S(2)}, u32[]{:S(2)}) collective-permute-start(bf16[2,2,64,256]{3,2,1,0:T(8,128)(2,1)S(1)} %get-tuple-element.30), channel_id=1, source_target_pairs={{0,12},{2,14},{4,8},{6,10},{8,4},{10,6},{12,0},{14,2},{16,28},{18,... | collective-permute-start | bytes 393224 | tf_op jit(solution)/shard_map/ppermute | solution.py:171
  53.7 0.2 shard_map.71.refs_6_
  53.9 0.2 collective-permute-done.24.refs_2_
  54.1 2.8 %collective-permute-done.25.refs_3_ = bf16[2,2,64,256]{3,2,1,0:T(8,128)(2,1)S(1)} collective-permute-done((bf16[2,2,64,256]{3,2,1,0:T(8,128)(2,1)S(1)}, bf16[2,2,64,256]{3,2,1,0:T(8,128)(2,1)S(1)}, u32[]{:S(2)}, u32[]{:S(2)}) %collective-permute-start.25) | collective-permute-done | bytes 131104 | tf_op jit(solution)/shard_map/ppermute | solution.py:171
  56.9 0.4 shard_map.70.refs_5_
  57.4 0.6 collective-permute-done.13.refs_1_
  58.0 1.8 %collective-permute-done.14.refs_2_ = bf16[2,2,64,256]{3,2,1,0:T(8,128)(2,1)S(1)} collective-permute-done((bf16[2,2,64,256]{3,2,1,0:T(8,128)(2,1)S(1)}, bf16[2,2,64,256]{3,2,1,0:T(8,128)(2,1)S(1)}, u32[]{:S(2)}, u32[]{:S(2)}) %collective-permute-start.14) | collective-permute-done | bytes 131104 | tf_op jit(solution)/shard_map/ppermute | solution.py:171
  59.8 1.9 %collective-permute-done.15.refs_3_ = bf16[2,2,64,256]{3,2,1,0:T(8,128)(2,1)S(1)} collective-permute-done((bf16[2,2,64,256]{3,2,1,0:T(8,128)(2,1)S(1)}, bf16[2,2,64,256]{3,2,1,0:T(8,128)(2,1)S(1)}, u32[]{:S(2)}, u32[]{:S(2)}) %collective-permute-start.15) | collective-permute-done | bytes 131104 | tf_op jit(solution)/shard_map/ppermute | solution.py:171
  61.7 1.3 %shard_map.72 = f32[256,1024]{1,0:T(8,128)} custom-call(bf16[2,2,64,256]{3,2,1,0:T(8,128)(2,1)S(1)} %get-tuple-element.27.refs_0_, bf16[2,2,64,256]{3,2,1,0:T(8,128)(2,1)S(1)} %collective-permute-done.13.refs_1_, bf16[2,2,64,256]{3,2,1,0:T(8,128)(2,1)S(1)} %collective-permute-done.14.refs_2_, bf16[2,2,64,256]{3,2,1,0:T(8,128)(2,1)S(1)} %collective-permute-done.15.refs_3_, ...), custom_call_target="tpu_custom_call" | custom-call | flops 268435456 | bytes 4194304 | tf_op jit(solution)/shard_map/pallas_call | solution.py:183
  (11 shorter events, 0.0 us)
Async XLA Ops:
  0.0 9.5 %collective-permute-start.4 = (bf16[64,2048]{1,0:T(8,128)(2,1)}, bf16[64,2048]{1,0:T(8,128)(2,1)S(1)}, u32[]{:S(2)}, u32[]{:S(2)}) collective-permute-start(bf16[64,2048]{1,0:T(8,128)(2,1)} %left.1), channel_id=1, source_target_pairs={{0,4},{2,6},{4,0},{6,2},{8,12},{10,14},{12,8},{14,10},{16,20},{18,... | collective-permute-start | bytes 786440 | tf_op jit(solution)/shard_map/ppermute | solution.py:171
  3.0 19.2 %collective-permute-start.3 = (bf16[64,2048]{1,0:T(8,128)(2,1)}, bf16[64,2048]{1,0:T(8,128)(2,1)S(1)}, u32[]{:S(2)}, u32[]{:S(2)}) collective-permute-start(bf16[64,2048]{1,0:T(8,128)(2,1)} %left.1), channel_id=1, source_target_pairs={{0,2},{2,0},{4,6},{6,4},{8,10},{10,8},{12,14},{14,12},{16,18},{18,... | collective-permute-start | bytes 786440 | tf_op jit(solution)/shard_map/ppermute | solution.py:171
  9.5 12.7 %collective-permute-start.5 = (bf16[64,2048]{1,0:T(8,128)(2,1)S(1)}, bf16[64,2048]{1,0:T(8,128)(2,1)S(1)}, u32[]{:S(2)}, u32[]{:S(2)}) collective-permute-start(bf16[64,2048]{1,0:T(8,128)(2,1)S(1)} %collective-permute-done.4.refs_2_), channel_id=1, source_target_pairs={{0,2},{2,0},{4,6},{6,4},{8,10},{10,8},{12,14},{14,12},{16,18},{18,... | collective-permute-start | bytes 786440 | tf_op jit(solution)/shard_map/ppermute | solution.py:171
  9.5 10.1 %collective-permute-start.1 = (bf16[32,2048]{1,0:T(8,128)(2,1)}, bf16[32,2048]{1,0:T(8,128)(2,1)S(1)}, u32[]{:S(2)}, u32[]{:S(2)}) collective-permute-start(bf16[32,2048]{1,0:T(8,128)(2,1)} %amplitudes.1), channel_id=1, source_target_pairs={{0,16},{2,18},{4,20},{6,22},{8,24},{10,26},{12,28},{14,30},{16,0},... | collective-permute-start | bytes 393224 | tf_op jit(solution)/shard_map/ppermute | solution.py:171
  12.3 21.0 %collective-permute-start = (bf16[32,2048]{1,0:T(8,128)(2,1)}, bf16[32,2048]{1,0:T(8,128)(2,1)S(1)}, u32[]{:S(2)}, u32[]{:S(2)}) collective-permute-start(bf16[32,2048]{1,0:T(8,128)(2,1)} %amplitudes.1), channel_id=1, source_target_pairs={{0,8},{2,10},{4,12},{6,14},{8,0},{10,2},{12,4},{14,6},{16,24},{18,... | collective-permute-start | bytes 393224 | tf_op jit(solution)/shard_map/ppermute | solution.py:171
  19.6 13.7 %collective-permute-start.2 = (bf16[32,2048]{1,0:T(8,128)(2,1)S(1)}, bf16[32,2048]{1,0:T(8,128)(2,1)S(1)}, u32[]{:S(2)}, u32[]{:S(2)}) collective-permute-start(bf16[32,2048]{1,0:T(8,128)(2,1)S(1)} %collective-permute-done.1.refs_0_), channel_id=1, source_target_pairs={{0,8},{2,10},{4,12},{6,14},{8,0},{10,2},{12,4},{14,6},{16,24},{18,... | collective-permute-start | bytes 393224 | tf_op jit(solution)/shard_map/ppermute | solution.py:171
  20.3 0.9 %copy-start.1 = (bf16[64,2048]{1,0:T(8,128)(2,1)S(1)}, bf16[64,2048]{1,0:T(8,128)(2,1)}, u32[]{:S(2)}) copy-start(bf16[64,2048]{1,0:T(8,128)(2,1)} %left.1) | copy-start | bytes 786436
  21.3 0.9 %copy-start.2 = (bf16[32,2048]{1,0:T(8,128)(2,1)S(1)}, bf16[32,2048]{1,0:T(8,128)(2,1)}, u32[]{:S(2)}) copy-start(bf16[32,2048]{1,0:T(8,128)(2,1)} %amplitudes.1) | copy-start | bytes 393220
  22.2 16.6 %copy-start.5 = (s32[8,32]{1,0:T(8,128)S(1)}, s32[8,32]{1,0:T(8,128)}, u32[]{:S(2)}) copy-start(s32[8,32]{1,0:T(8,128)} %param.9) | copy-start | bytes 3076
  22.8 30.8 %copy-start.3 = (f32[1024]{0:T(1024)S(1)}, f32[1024]{0:T(1024)}, u32[]{:S(2)}) copy-start(f32[1024]{0:T(1024)} %param.11) | copy-start | bytes 12292
  22.8 30.8 %copy-start.4 = (f32[256]{0:T(256)S(1)}, f32[256]{0:T(256)}, u32[]{:S(2)}) copy-start(f32[256]{0:T(256)} %param.10) | copy-start | bytes 3076
  22.8 6.7 %collective-permute-start.19 = (bf16[4,32,256]{2,1,0:T(8,128)(2,1)S(1)}, bf16[4,32,256]{2,1,0:T(8,128)(2,1)S(1)}, u32[]{:S(2)}, u32[]{:S(2)}) collective-permute-start(bf16[4,32,256]{2,1,0:T(8,128)(2,1)S(1)} %get-tuple-element.33), channel_id=1, source_target_pairs={{0,16},{1,17},{2,18},{3,19},{4,20},{5,21},{6,22},{7,23},{8,24},{9,... | collective-permute-start | bytes 196616 | tf_op jit(solution)/shard_map/ppermute | solution.py:179
  26.2 7.1 %collective-permute-start.20 = (bf16[4,32,256]{2,1,0:T(8,128)(2,1)S(1)}, bf16[4,32,256]{2,1,0:T(8,128)(2,1)S(1)}, u32[]{:S(2)}, u32[]{:S(2)}) collective-permute-start(bf16[4,32,256]{2,1,0:T(8,128)(2,1)S(1)} %get-tuple-element.34), channel_id=1, source_target_pairs={{0,17},{1,16},{2,19},{3,18},{4,21},{5,20},{6,23},{7,22},{8,25},{9,... | collective-permute-start | bytes 196616 | tf_op jit(solution)/shard_map/ppermute | solution.py:179
  27.2 11.1 %collective-permute-start.16 = (f32[4,32,256]{2,1,0:T(8,128)S(1)}, f32[4,32,256]{2,1,0:T(8,128)S(1)}, u32[]{:S(2)}, u32[]{:S(2)}) collective-permute-start(f32[4,32,256]{2,1,0:T(8,128)S(1)} %get-tuple-element.32), channel_id=1, source_target_pairs={{0,1},{1,0},{2,3},{3,2},{4,5},{5,4},{6,7},{7,6},{8,9},{9,8},{10,11... | collective-permute-start | bytes 393224 | tf_op jit(solution)/shard_map/ppermute | solution.py:171
  29.5 7.5 %collective-permute-start.21 = (bf16[4,32,256]{2,1,0:T(8,128)(2,1)S(1)}, bf16[4,32,256]{2,1,0:T(8,128)(2,1)S(1)}, u32[]{:S(2)}, u32[]{:S(2)}) collective-permute-start(bf16[4,32,256]{2,1,0:T(8,128)(2,1)S(1)} %collective-permute-done.19.refs_4_), channel_id=1, source_target_pairs={{0,2},{2,0},{4,6},{6,4},{8,10},{10,8},{12,14},{14,12},{16,18},{18,... | collective-permute-start | bytes 196616 | tf_op jit(solution)/shard_map/ppermute | solution.py:171
  33.3 5.0 %collective-permute-start.22 = (bf16[4,32,256]{2,1,0:T(8,128)(2,1)S(1)}, bf16[4,32,256]{2,1,0:T(8,128)(2,1)S(1)}, u32[]{:S(2)}, u32[]{:S(2)}) collective-permute-start(bf16[4,32,256]{2,1,0:T(8,128)(2,1)S(1)} %collective-permute-done.20.refs_5_), channel_id=1, source_target_pairs={{0,2},{2,0},{4,6},{6,4},{8,10},{10,8},{12,14},{14,12},{16,18},{18,... | collective-permute-start | bytes 196616 | tf_op jit(solution)/shard_map/ppermute | solution.py:171
  33.4 23.5 %copy-start = (bf16[1024,1024]{1,0:T(8,128)(2,1)S(1)}, bf16[1024,1024]{1,0:T(8,128)(2,1)}, u32[]{:S(2)}) copy-start(bf16[1024,1024]{1,0:T(8,128)(2,1)} %refs_4_.3) | copy-start | bytes 6291460
  33.8 12.6 %collective-permute-start.9 = (bf16[4,32,256]{2,1,0:T(8,128)(2,1)S(1)}, bf16[4,32,256]{2,1,0:T(8,128)(2,1)S(1)}, u32[]{:S(2)}, u32[]{:S(2)}) collective-permute-start(bf16[4,32,256]{2,1,0:T(8,128)(2,1)S(1)} %get-tuple-element.25), channel_id=1, source_target_pairs={{0,16},{1,17},{2,18},{3,19},{4,20},{5,21},{6,22},{7,23},{8,24},{9,... | collective-permute-start | bytes 196616 | tf_op jit(solution)/shard_map/ppermute | solution.py:179
  34.0 12.5 %collective-permute-start.10 = (bf16[4,32,256]{2,1,0:T(8,128)(2,1)S(1)}, bf16[4,32,256]{2,1,0:T(8,128)(2,1)S(1)}, u32[]{:S(2)}, u32[]{:S(2)}) collective-permute-start(bf16[4,32,256]{2,1,0:T(8,128)(2,1)S(1)} %get-tuple-element.26), channel_id=1, source_target_pairs={{0,17},{1,16},{2,19},{3,18},{4,21},{5,20},{6,23},{7,22},{8,25},{9,... | collective-permute-start | bytes 196616 | tf_op jit(solution)/shard_map/ppermute | solution.py:179
  37.0 6.7 %collective-permute-start.6 = (f32[4,32,256]{2,1,0:T(8,128)S(1)}, f32[4,32,256]{2,1,0:T(8,128)S(1)}, u32[]{:S(2)}, u32[]{:S(2)}) collective-permute-start(f32[4,32,256]{2,1,0:T(8,128)S(1)} %get-tuple-element.24), channel_id=1, source_target_pairs={{0,1},{1,0},{2,3},{3,2},{4,5},{5,4},{6,7},{7,6},{8,9},{9,8},{10,11... | collective-permute-start | bytes 393224 | tf_op jit(solution)/shard_map/ppermute | solution.py:171
  38.3 5.5 %collective-permute-start.17 = (f32[4,32,256]{2,1,0:T(8,128)S(1)}, f32[4,32,256]{2,1,0:T(8,128)S(1)}, u32[]{:S(2)}, u32[]{:S(2)}) collective-permute-start(f32[4,32,256]{2,1,0:T(8,128)S(1)} %get-tuple-element.31.refs_0_), channel_id=1, source_target_pairs={{0,2},{2,0},{4,6},{6,4},{8,10},{10,8},{12,14},{14,12},{16,18},{18,... | collective-permute-start | bytes 393224 | tf_op jit(solution)/shard_map/ppermute | solution.py:171
  38.3 6.2 %collective-permute-start.18 = (f32[4,32,256]{2,1,0:T(8,128)S(1)}, f32[4,32,256]{2,1,0:T(8,128)S(1)}, u32[]{:S(2)}, u32[]{:S(2)}) collective-permute-start(f32[4,32,256]{2,1,0:T(8,128)S(1)} %collective-permute-done.16.refs_1_), channel_id=1, source_target_pairs={{0,2},{2,0},{4,6},{6,4},{8,10},{10,8},{12,14},{14,12},{16,18},{18,... | collective-permute-start | bytes 393224 | tf_op jit(solution)/shard_map/ppermute | solution.py:171
  43.8 5.9 %collective-permute-start.7 = (f32[4,32,256]{2,1,0:T(8,128)S(1)}, f32[4,32,256]{2,1,0:T(8,128)S(1)}, u32[]{:S(2)}, u32[]{:S(2)}) collective-permute-start(f32[4,32,256]{2,1,0:T(8,128)S(1)} %get-tuple-element.23.refs_0_), channel_id=1, source_target_pairs={{0,2},{2,0},{4,6},{6,4},{8,10},{10,8},{12,14},{14,12},{16,18},{18,... | collective-permute-start | bytes 393224 | tf_op jit(solution)/shard_map/ppermute | solution.py:171
  43.8 5.9 %collective-permute-start.8 = (f32[4,32,256]{2,1,0:T(8,128)S(1)}, f32[4,32,256]{2,1,0:T(8,128)S(1)}, u32[]{:S(2)}, u32[]{:S(2)}) collective-permute-start(f32[4,32,256]{2,1,0:T(8,128)S(1)} %collective-permute-done.6.refs_1_), channel_id=1, source_target_pairs={{0,2},{2,0},{4,6},{6,4},{8,10},{10,8},{12,14},{14,12},{16,18},{18,... | collective-permute-start | bytes 393224 | tf_op jit(solution)/shard_map/ppermute | solution.py:171
  44.9 7.2 %collective-permute-start.23 = (bf16[2,2,64,256]{3,2,1,0:T(8,128)(2,1)S(1)}, bf16[2,2,64,256]{3,2,1,0:T(8,128)(2,1)S(1)}, u32[]{:S(2)}, u32[]{:S(2)}) collective-permute-start(bf16[2,2,64,256]{3,2,1,0:T(8,128)(2,1)S(1)} %get-tuple-element.36), channel_id=1, source_target_pairs={{0,4},{2,6},{4,0},{6,2},{8,12},{10,14},{12,8},{14,10},{16,20},{18,... | collective-permute-start | bytes 393224 | tf_op jit(solution)/shard_map/ppermute | solution.py:171
  46.5 1.3 %collective-permute-start.11 = (bf16[4,32,256]{2,1,0:T(8,128)(2,1)S(1)}, bf16[4,32,256]{2,1,0:T(8,128)(2,1)S(1)}, u32[]{:S(2)}, u32[]{:S(2)}) collective-permute-start(bf16[4,32,256]{2,1,0:T(8,128)(2,1)S(1)} %collective-permute-done.9.refs_4_), channel_id=1, source_target_pairs={{0,2},{2,0},{4,6},{6,4},{8,10},{10,8},{12,14},{14,12},{16,18},{18,... | collective-permute-start | bytes 196616 | tf_op jit(solution)/shard_map/ppermute | solution.py:171
  46.5 1.6 %collective-permute-start.12 = (bf16[4,32,256]{2,1,0:T(8,128)(2,1)S(1)}, bf16[4,32,256]{2,1,0:T(8,128)(2,1)S(1)}, u32[]{:S(2)}, u32[]{:S(2)}) collective-permute-start(bf16[4,32,256]{2,1,0:T(8,128)(2,1)S(1)} %collective-permute-done.10.refs_5_), channel_id=1, source_target_pairs={{0,2},{2,0},{4,6},{6,4},{8,10},{10,8},{12,14},{14,12},{16,18},{18,... | collective-permute-start | bytes 196616 | tf_op jit(solution)/shard_map/ppermute | solution.py:171
  47.7 6.4 %collective-permute-start.24 = (bf16[2,2,64,256]{3,2,1,0:T(8,128)(2,1)S(1)}, bf16[2,2,64,256]{3,2,1,0:T(8,128)(2,1)S(1)}, u32[]{:S(2)}, u32[]{:S(2)}) collective-permute-start(bf16[2,2,64,256]{3,2,1,0:T(8,128)(2,1)S(1)} %get-tuple-element.37), channel_id=1, source_target_pairs={{0,8},{2,10},{4,12},{6,14},{8,0},{10,2},{12,4},{14,6},{16,24},{18,... | collective-permute-start | bytes 393224 | tf_op jit(solution)/shard_map/ppermute | solution.py:171
  48.1 8.8 %collective-permute-start.25 = (bf16[2,2,64,256]{3,2,1,0:T(8,128)(2,1)S(1)}, bf16[2,2,64,256]{3,2,1,0:T(8,128)(2,1)S(1)}, u32[]{:S(2)}, u32[]{:S(2)}) collective-permute-start(bf16[2,2,64,256]{3,2,1,0:T(8,128)(2,1)S(1)} %get-tuple-element.38), channel_id=1, source_target_pairs={{0,12},{2,14},{4,8},{6,10},{8,4},{10,6},{12,0},{14,2},{16,28},{18,... | collective-permute-start | bytes 393224 | tf_op jit(solution)/shard_map/ppermute | solution.py:171
  50.1 7.9 %collective-permute-start.13 = (bf16[2,2,64,256]{3,2,1,0:T(8,128)(2,1)S(1)}, bf16[2,2,64,256]{3,2,1,0:T(8,128)(2,1)S(1)}, u32[]{:S(2)}, u32[]{:S(2)}) collective-permute-start(bf16[2,2,64,256]{3,2,1,0:T(8,128)(2,1)S(1)} %get-tuple-element.28), channel_id=1, source_target_pairs={{0,4},{2,6},{4,0},{6,2},{8,12},{10,14},{12,8},{14,10},{16,20},{18,... | collective-permute-start | bytes 393224 | tf_op jit(solution)/shard_map/ppermute | solution.py:171
  51.7 8.1 %collective-permute-start.14 = (bf16[2,2,64,256]{3,2,1,0:T(8,128)(2,1)S(1)}, bf16[2,2,64,256]{3,2,1,0:T(8,128)(2,1)S(1)}, u32[]{:S(2)}, u32[]{:S(2)}) collective-permute-start(bf16[2,2,64,256]{3,2,1,0:T(8,128)(2,1)S(1)} %get-tuple-element.29), channel_id=1, source_target_pairs={{0,8},{2,10},{4,12},{6,14},{8,0},{10,2},{12,4},{14,6},{16,24},{18,... | collective-permute-start | bytes 393224 | tf_op jit(solution)/shard_map/ppermute | solution.py:171
  52.0 9.7 %collective-permute-start.15 = (bf16[2,2,64,256]{3,2,1,0:T(8,128)(2,1)S(1)}, bf16[2,2,64,256]{3,2,1,0:T(8,128)(2,1)S(1)}, u32[]{:S(2)}, u32[]{:S(2)}) collective-permute-start(bf16[2,2,64,256]{3,2,1,0:T(8,128)(2,1)S(1)} %get-tuple-element.30), channel_id=1, source_target_pairs={{0,12},{2,14},{4,8},{6,10},{8,4},{10,6},{12,0},{14,2},{16,28},{18,... | collective-permute-start | bytes 393224 | tf_op jit(solution)/shard_map/ppermute | solution.py:171
where the time goes:
time: 63.2 us; the launch traced here: 63 us
  waiting for transfers between devices  30.9 us (49%)
  starting transfers between devices  26.1 us (41%)
  Pallas kernels  3.87 us (6%)
  local copies, waits for them, and re-layouts  1.96 us (3%)
    ppermute x22, waiting for transfers between devices, swap(): return lax.ppermute(value, axis, [(t, t ^ q) for t in range(size)])  25.3 us
    ppermute x22, starting transfers between devices, swap(): return lax.ppermute(value, axis, [(t, t ^ q) for t in range(size)])  18.5 us
    ppermute x4, starting transfers between devices, cross(): return lax.ppermute(value, ('tile', 'inner'), pairs)  7.55 us
    ppermute x4, waiting for transfers between devices, cross(): return lax.ppermute(value, ('tile', 'inner'), pairs)  5.6 us
    pallas_call x9, Pallas kernels, call(): pl.pallas_call(kernel, out_shape=out_shape, in_specs=in_specs, out_specs=...  3.87 us
    unnamed x12, local copies, waits for them, and re-layouts  1.88 us
  transfers between devices with their start and end apart: 26, of which 11 were waited for; matrix products, arithmetic and copies ran while one was open for 0% of the time, Pallas kernels for 4%

commit v1 on v0

--- a/solution.py
+++ b/solution.py
@@ -134,8 +134,9 @@
     z, y, core, _ = place()
     right_tiles, _, both, depth = t_refs[0].shape
     low, rows = lax.rem(z, parts), both // 2
-    for d in range(right_tiles):
-        cols = slice(d * TILE, (d + 1) * TILE)
+    piece = TILE // 2
+    for k in range(2 * right_tiles):
+        d, cols = k // 2, slice(k * piece, (k + 1) * piece)
         for o in range(parts):
             here = slice(o * 2 * both, (o + 1) * 2 * both)
             total = None if so_far is None else so_far[here, cols]
@@ -155,11 +156,11 @@
                 at = pl.ds(pl.multiple_of(at, rows), rows)
                 staged[at, cols] = total[i * rows : (i + 1) * rows, :] * inverse[at, cols]
         if last:
-            pltpu.make_async_copy(staged.at[:, cols], out.at[:, cols], sem.at[d]).start()
+            pltpu.make_async_copy(staged.at[:, cols], out.at[:, cols], sem.at[k]).start()
     if last:
-        for d in range(right_tiles):
-            cols = slice(d * TILE, (d + 1) * TILE)
-            pltpu.make_async_copy(staged.at[:, cols], out.at[:, cols], sem.at[d]).wait()
+        for k in range(2 * right_tiles):
+            cols = slice(k * piece, (k + 1) * piece)
+            pltpu.make_async_copy(staged.at[:, cols], out.at[:, cols], sem.at[k]).wait()
 
 
 def solution(mesh):
@@ -287,7 +288,7 @@
                     operands,
                     [VMEM] * len(operands),
                     jax.ShapeDtypeStruct(result_shape, jnp.float32) if last else pltpu.VMEM(result_shape, jnp.float32),
-                    [pltpu.VMEM(result_shape, jnp.float32), pltpu.SemaphoreType.DMA((right_tiles,))] if last else (),
+                    [pltpu.VMEM(result_shape, jnp.float32), pltpu.SemaphoreType.DMA((2 * right_tiles,))] if last else (),
                     2 * occupied_shift.shape[0] * out_width * right_factors.shape[0] // parts,
                     4 << 20,
                 ),

time: 63.2 us -> 63.1 us (level)
  no operation moved by 1% of the time
where the time goes in v1:
time: 63.1 us; the launch traced here: 63 us
  waiting for transfers between devices  30.9 us (49%)
  starting transfers between devices  26.1 us (41%)
  Pallas kernels  3.85 us (6%)
  local copies, waits for them, and re-layouts  1.96 us (3%)
    ppermute x22, waiting for transfers between devices, swap(): return lax.ppermute(value, axis, [(t, t ^ q) for t in range(size)])  25.3 us
    ppermute x22, starting transfers between devices, swap(): return lax.ppermute(value, axis, [(t, t ^ q) for t in range(size)])  18.5 us
    ppermute x4, starting transfers between devices, cross(): return lax.ppermute(value, ('tile', 'inner'), pairs)  7.55 us
    ppermute x4, waiting for transfers between devices, cross(): return lax.ppermute(value, ('tile', 'inner'), pairs)  5.6 us
    pallas_call x9, Pallas kernels, call(): pl.pallas_call(kernel, out_shape=out_shape, in_specs=in_specs, out_specs=...  3.85 us
    unnamed x12, local copies, waits for them, and re-layouts  1.88 us
  transfers between devices with their start and end apart: 26, of which 11 were waited for; matrix products, arithmetic and copies ran while one was open for 0% of the time, Pallas kernels for 4%

profile of v1, /device:TPU:0, one launch (start us, length us, event | category | flops | bytes accessed | tf_op | source)
XLA Modules:
  0.0 63.0 jit_solution(15094845436597732118)
XLA Ops:
  0.0 3.0 %collective-permute-start.4 = (bf16[64,2048]{1,0:T(8,128)(2,1)}, bf16[64,2048]{1,0:T(8,128)(2,1)S(1)}, u32[]{:S(2)}, u32[]{:S(2)}) collective-permute-start(bf16[64,2048]{1,0:T(8,128)(2,1)} %left.1), channel_id=1, source_target_pairs={{0,4},{2,6},{4,0},{6,2},{8,12},{10,14},{12,8},{14,10},{16,20},{18,... | collective-permute-start | bytes 786440 | tf_op jit(solution)/shard_map/ppermute | solution.py:172
  3.0 0.0 collective-permute-start.3
  3.0 6.5 %collective-permute-done.4.refs_2_ = bf16[64,2048]{1,0:T(8,128)(2,1)S(1)} collective-permute-done((bf16[64,2048]{1,0:T(8,128)(2,1)}, bf16[64,2048]{1,0:T(8,128)(2,1)S(1)}, u32[]{:S(2)}, u32[]{:S(2)}) %collective-permute-start.4) | collective-permute-done | bytes 262176 | tf_op jit(solution)/shard_map/ppermute | solution.py:172
  9.5 0.0 collective-permute-start.5
  9.5 2.8 %collective-permute-start.1 = (bf16[32,2048]{1,0:T(8,128)(2,1)}, bf16[32,2048]{1,0:T(8,128)(2,1)S(1)}, u32[]{:S(2)}, u32[]{:S(2)}) collective-permute-start(bf16[32,2048]{1,0:T(8,128)(2,1)} %amplitudes.1), channel_id=1, source_target_pairs={{0,16},{2,18},{4,20},{6,22},{8,24},{10,26},{12,28},{14,30},{16,0},... | collective-permute-start | bytes 393224 | tf_op jit(solution)/shard_map/ppermute | solution.py:172
  12.3 1.6 %collective-permute-start = (bf16[32,2048]{1,0:T(8,128)(2,1)}, bf16[32,2048]{1,0:T(8,128)(2,1)S(1)}, u32[]{:S(2)}, u32[]{:S(2)}) collective-permute-start(bf16[32,2048]{1,0:T(8,128)(2,1)} %amplitudes.1), channel_id=1, source_target_pairs={{0,8},{2,10},{4,12},{6,14},{8,0},{10,2},{12,4},{14,6},{16,24},{18,... | collective-permute-start | bytes 393224 | tf_op jit(solution)/shard_map/ppermute | solution.py:172
  13.9 5.7 %collective-permute-done.1.refs_0_ = bf16[32,2048]{1,0:T(8,128)(2,1)S(1)} collective-permute-done((bf16[32,2048]{1,0:T(8,128)(2,1)}, bf16[32,2048]{1,0:T(8,128)(2,1)S(1)}, u32[]{:S(2)}, u32[]{:S(2)}) %collective-permute-start.1) | collective-permute-done | bytes 131104 | tf_op jit(solution)/shard_map/ppermute | solution.py:172
  19.6 0.7 %collective-permute-start.2 = (bf16[32,2048]{1,0:T(8,128)(2,1)S(1)}, bf16[32,2048]{1,0:T(8,128)(2,1)S(1)}, u32[]{:S(2)}, u32[]{:S(2)}) collective-permute-start(bf16[32,2048]{1,0:T(8,128)(2,1)S(1)} %collective-permute-done.1.refs_0_), channel_id=1, source_target_pairs={{0,8},{2,10},{4,12},{6,14},{8,0},{10,2},{12,4},{14,6},{16,24},{18,... | collective-permute-start | bytes 393224 | tf_op jit(solution)/shard_map/ppermute | solution.py:172
  20.3 0.9 %copy-done.1 = bf16[64,2048]{1,0:T(8,128)(2,1)S(1)} copy-done((bf16[64,2048]{1,0:T(8,128)(2,1)S(1)}, bf16[64,2048]{1,0:T(8,128)(2,1)}, u32[]{:S(2)}) %copy-start.1) | copy-done | bytes 262168
  21.3 0.9 %copy-done.2 = bf16[32,2048]{1,0:T(8,128)(2,1)S(1)} copy-done((bf16[32,2048]{1,0:T(8,128)(2,1)S(1)}, bf16[32,2048]{1,0:T(8,128)(2,1)}, u32[]{:S(2)}) %copy-start.2) | copy-done | bytes 131096
  22.2 0.0 collective-permute-done.3.refs_1_
  22.2 0.0 collective-permute-done.5.refs_3_
  22.2 0.6 shard_map.66
  22.8 0.0 copy-start.3
  22.8 0.0 copy-start.4
  22.8 3.3 %collective-permute-start.19 = (bf16[4,32,256]{2,1,0:T(8,128)(2,1)S(1)}, bf16[4,32,256]{2,1,0:T(8,128)(2,1)S(1)}, u32[]{:S(2)}, u32[]{:S(2)}) collective-permute-start(bf16[4,32,256]{2,1,0:T(8,128)(2,1)S(1)} %get-tuple-element.33), channel_id=1, source_target_pairs={{0,16},{1,17},{2,18},{3,19},{4,20},{5,21},{6,22},{7,23},{8,24},{9,... | collective-permute-start | bytes 196616 | tf_op jit(solution)/shard_map/ppermute | solution.py:180
  26.2 1.0 %collective-permute-start.20 = (bf16[4,32,256]{2,1,0:T(8,128)(2,1)S(1)}, bf16[4,32,256]{2,1,0:T(8,128)(2,1)S(1)}, u32[]{:S(2)}, u32[]{:S(2)}) collective-permute-start(bf16[4,32,256]{2,1,0:T(8,128)(2,1)S(1)} %get-tuple-element.34), channel_id=1, source_target_pairs={{0,17},{1,16},{2,19},{3,18},{4,21},{5,20},{6,23},{7,22},{8,25},{9,... | collective-permute-start | bytes 196616 | tf_op jit(solution)/shard_map/ppermute | solution.py:180
  27.2 0.5 collective-permute-start.16
  27.7 1.8 %collective-permute-done.19.refs_4_ = bf16[4,32,256]{2,1,0:T(8,128)(2,1)S(1)} collective-permute-done((bf16[4,32,256]{2,1,0:T(8,128)(2,1)S(1)}, bf16[4,32,256]{2,1,0:T(8,128)(2,1)S(1)}, u32[]{:S(2)}, u32[]{:S(2)}) %collective-permute-start.19) | collective-permute-done | bytes 65568 | tf_op jit(solution)/shard_map/ppermute | solution.py:180
  29.5 0.0 collective-permute-start.21
  29.5 3.8 %collective-permute-done.20.refs_5_ = bf16[4,32,256]{2,1,0:T(8,128)(2,1)S(1)} collective-permute-done((bf16[4,32,256]{2,1,0:T(8,128)(2,1)S(1)}, bf16[4,32,256]{2,1,0:T(8,128)(2,1)S(1)}, u32[]{:S(2)}, u32[]{:S(2)}) %collective-permute-start.20) | collective-permute-done | bytes 65568 | tf_op jit(solution)/shard_map/ppermute | solution.py:180
  33.3 0.0 collective-permute-start.22
  33.3 0.0 collective-permute-done.refs_0_
  33.3 0.0 collective-permute-done.2.refs_1_
  33.4 0.0 copy-start
  33.4 0.5 shard_map.67
  33.8 0.1 collective-permute-start.9
  34.0 3.1 %collective-permute-start.10 = (bf16[4,32,256]{2,1,0:T(8,128)(2,1)S(1)}, bf16[4,32,256]{2,1,0:T(8,128)(2,1)S(1)}, u32[]{:S(2)}, u32[]{:S(2)}) collective-permute-start(bf16[4,32,256]{2,1,0:T(8,128)(2,1)S(1)} %get-tuple-element.26), channel_id=1, source_target_pairs={{0,17},{1,16},{2,19},{3,18},{4,21},{5,20},{6,23},{7,22},{8,25},{9,... | collective-permute-start | bytes 196616 | tf_op jit(solution)/shard_map/ppermute | solution.py:180
  37.0 0.0 collective-permute-done.21.refs_6_
  37.0 1.3 %collective-permute-start.6 = (f32[4,32,256]{2,1,0:T(8,128)S(1)}, f32[4,32,256]{2,1,0:T(8,128)S(1)}, u32[]{:S(2)}, u32[]{:S(2)}) collective-permute-start(f32[4,32,256]{2,1,0:T(8,128)S(1)} %get-tuple-element.24), channel_id=1, source_target_pairs={{0,1},{1,0},{2,3},{3,2},{4,5},{5,4},{6,7},{7,6},{8,9},{9,8},{10,11... | collective-permute-start | bytes 393224 | tf_op jit(solution)/shard_map/ppermute | solution.py:172
  38.3 0.0 collective-permute-done.22.refs_7_
  38.3 0.0 collective-permute-start.17
  38.3 0.0 collective-permute-done.16.refs_1_
  38.3 0.5 collective-permute-start.18
  38.8 5.0 %collective-permute-done.6.refs_1_ = f32[4,32,256]{2,1,0:T(8,128)S(1)} collective-permute-done((f32[4,32,256]{2,1,0:T(8,128)S(1)}, f32[4,32,256]{2,1,0:T(8,128)S(1)}, u32[]{:S(2)}, u32[]{:S(2)}) %collective-permute-start.6) | collective-permute-done | bytes 131104 | tf_op jit(solution)/shard_map/ppermute | solution.py:172
  43.8 0.0 collective-permute-start.7
  43.8 0.0 collective-permute-done.17.refs_2_
  43.8 0.5 collective-permute-start.8
  44.3 0.1 broadcast_in_dim.2.mask
  44.4 0.1 shard_map.64.weights
  44.5 0.0 collective-permute-done.18.refs_3_
  44.5 0.4 shard_map.69
  44.9 1.6 %collective-permute-start.23 = (bf16[2,2,64,256]{3,2,1,0:T(8,128)(2,1)S(1)}, bf16[2,2,64,256]{3,2,1,0:T(8,128)(2,1)S(1)}, u32[]{:S(2)}, u32[]{:S(2)}) collective-permute-start(bf16[2,2,64,256]{3,2,1,0:T(8,128)(2,1)S(1)} %get-tuple-element.36), channel_id=1, source_target_pairs={{0,4},{2,6},{4,0},{6,2},{8,12},{10,14},{12,8},{14,10},{16,20},{18,... | collective-permute-start | bytes 393224 | tf_op jit(solution)/shard_map/ppermute | solution.py:172
  46.5 0.0 collective-permute-done.9.refs_4_
  46.5 0.0 collective-permute-start.11
  46.5 0.0 collective-permute-done.10.refs_5_
  46.5 0.5 collective-permute-start.12
  47.0 0.7 %collective-permute-done.11.refs_6_ = bf16[4,32,256]{2,1,0:T(8,128)(2,1)S(1)} collective-permute-done((bf16[4,32,256]{2,1,0:T(8,128)(2,1)S(1)}, bf16[4,32,256]{2,1,0:T(8,128)(2,1)S(1)}, u32[]{:S(2)}, u32[]{:S(2)}) %collective-permute-start.11) | collective-permute-done | bytes 65568 | tf_op jit(solution)/shard_map/ppermute | solution.py:172
  47.7 0.4 collective-permute-start.24
  48.1 0.0 collective-permute-done.12.refs_7_
  48.1 1.6 %collective-permute-start.25 = (bf16[2,2,64,256]{3,2,1,0:T(8,128)(2,1)S(1)}, bf16[2,2,64,256]{3,2,1,0:T(8,128)(2,1)S(1)}, u32[]{:S(2)}, u32[]{:S(2)}) collective-permute-start(bf16[2,2,64,256]{3,2,1,0:T(8,128)(2,1)S(1)} %get-tuple-element.38), channel_id=1, source_target_pairs={{0,12},{2,14},{4,8},{6,10},{8,4},{10,6},{12,0},{14,2},{16,28},{18,... | collective-permute-start | bytes 393224 | tf_op jit(solution)/shard_map/ppermute | solution.py:172
  49.7 0.4 shard_map.68
  50.1 1.6 %collective-permute-start.13 = (bf16[2,2,64,256]{3,2,1,0:T(8,128)(2,1)S(1)}, bf16[2,2,64,256]{3,2,1,0:T(8,128)(2,1)S(1)}, u32[]{:S(2)}, u32[]{:S(2)}) collective-permute-start(bf16[2,2,64,256]{3,2,1,0:T(8,128)(2,1)S(1)} %get-tuple-element.28), channel_id=1, source_target_pairs={{0,4},{2,6},{4,0},{6,2},{8,12},{10,14},{12,8},{14,10},{16,20},{18,... | collective-permute-start | bytes 393224 | tf_op jit(solution)/shard_map/ppermute | solution.py:172
  51.7 0.4 collective-permute-start.14
  52.0 0.0 collective-permute-done.23.refs_1_
  52.0 1.6 %collective-permute-start.15 = (bf16[2,2,64,256]{3,2,1,0:T(8,128)(2,1)S(1)}, bf16[2,2,64,256]{3,2,1,0:T(8,128)(2,1)S(1)}, u32[]{:S(2)}, u32[]{:S(2)}) collective-permute-start(bf16[2,2,64,256]{3,2,1,0:T(8,128)(2,1)S(1)} %get-tuple-element.30), channel_id=1, source_target_pairs={{0,12},{2,14},{4,8},{6,10},{8,4},{10,6},{12,0},{14,2},{16,28},{18,... | collective-permute-start | bytes 393224 | tf_op jit(solution)/shard_map/ppermute | solution.py:172
  53.7 0.2 shard_map.71.refs_6_
  53.9 0.2 collective-permute-done.24.refs_2_
  54.1 2.8 %collective-permute-done.25.refs_3_ = bf16[2,2,64,256]{3,2,1,0:T(8,128)(2,1)S(1)} collective-permute-done((bf16[2,2,64,256]{3,2,1,0:T(8,128)(2,1)S(1)}, bf16[2,2,64,256]{3,2,1,0:T(8,128)(2,1)S(1)}, u32[]{:S(2)}, u32[]{:S(2)}) %collective-permute-start.25) | collective-permute-done | bytes 131104 | tf_op jit(solution)/shard_map/ppermute | solution.py:172
  56.9 0.4 shard_map.70.refs_5_
  57.4 0.6 collective-permute-done.13.refs_1_
  58.0 1.8 %collective-permute-done.14.refs_2_ = bf16[2,2,64,256]{3,2,1,0:T(8,128)(2,1)S(1)} collective-permute-done((bf16[2,2,64,256]{3,2,1,0:T(8,128)(2,1)S(1)}, bf16[2,2,64,256]{3,2,1,0:T(8,128)(2,1)S(1)}, u32[]{:S(2)}, u32[]{:S(2)}) %collective-permute-start.14) | collective-permute-done | bytes 131104 | tf_op jit(solution)/shard_map/ppermute | solution.py:172
  59.8 1.9 %collective-permute-done.15.refs_3_ = bf16[2,2,64,256]{3,2,1,0:T(8,128)(2,1)S(1)} collective-permute-done((bf16[2,2,64,256]{3,2,1,0:T(8,128)(2,1)S(1)}, bf16[2,2,64,256]{3,2,1,0:T(8,128)(2,1)S(1)}, u32[]{:S(2)}, u32[]{:S(2)}) %collective-permute-start.15) | collective-permute-done | bytes 131104 | tf_op jit(solution)/shard_map/ppermute | solution.py:172
  61.7 1.3 %shard_map.72 = f32[256,1024]{1,0:T(8,128)} custom-call(bf16[2,2,64,256]{3,2,1,0:T(8,128)(2,1)S(1)} %get-tuple-element.27.refs_0_, bf16[2,2,64,256]{3,2,1,0:T(8,128)(2,1)S(1)} %collective-permute-done.13.refs_1_, bf16[2,2,64,256]{3,2,1,0:T(8,128)(2,1)S(1)} %collective-permute-done.14.refs_2_, bf16[2,2,64,256]{3,2,1,0:T(8,128)(2,1)S(1)} %collective-permute-done.15.refs_3_, ...), custom_call_target="tpu_custom_call" | custom-call | flops 268435456 | bytes 4194304 | tf_op jit(solution)/shard_map/pallas_call | solution.py:184
  (11 shorter events, 0.0 us)
Async XLA Ops:
  0.0 9.5 %collective-permute-start.4 = (bf16[64,2048]{1,0:T(8,128)(2,1)}, bf16[64,2048]{1,0:T(8,128)(2,1)S(1)}, u32[]{:S(2)}, u32[]{:S(2)}) collective-permute-start(bf16[64,2048]{1,0:T(8,128)(2,1)} %left.1), channel_id=1, source_target_pairs={{0,4},{2,6},{4,0},{6,2},{8,12},{10,14},{12,8},{14,10},{16,20},{18,... | collective-permute-start | bytes 786440 | tf_op jit(solution)/shard_map/ppermute | solution.py:172
  3.0 19.2 %collective-permute-start.3 = (bf16[64,2048]{1,0:T(8,128)(2,1)}, bf16[64,2048]{1,0:T(8,128)(2,1)S(1)}, u32[]{:S(2)}, u32[]{:S(2)}) collective-permute-start(bf16[64,2048]{1,0:T(8,128)(2,1)} %left.1), channel_id=1, source_target_pairs={{0,2},{2,0},{4,6},{6,4},{8,10},{10,8},{12,14},{14,12},{16,18},{18,... | collective-permute-start | bytes 786440 | tf_op jit(solution)/shard_map/ppermute | solution.py:172
  9.5 12.7 %collective-permute-start.5 = (bf16[64,2048]{1,0:T(8,128)(2,1)S(1)}, bf16[64,2048]{1,0:T(8,128)(2,1)S(1)}, u32[]{:S(2)}, u32[]{:S(2)}) collective-permute-start(bf16[64,2048]{1,0:T(8,128)(2,1)S(1)} %collective-permute-done.4.refs_2_), channel_id=1, source_target_pairs={{0,2},{2,0},{4,6},{6,4},{8,10},{10,8},{12,14},{14,12},{16,18},{18,... | collective-permute-start | bytes 786440 | tf_op jit(solution)/shard_map/ppermute | solution.py:172
  9.5 10.1 %collective-permute-start.1 = (bf16[32,2048]{1,0:T(8,128)(2,1)}, bf16[32,2048]{1,0:T(8,128)(2,1)S(1)}, u32[]{:S(2)}, u32[]{:S(2)}) collective-permute-start(bf16[32,2048]{1,0:T(8,128)(2,1)} %amplitudes.1), channel_id=1, source_target_pairs={{0,16},{2,18},{4,20},{6,22},{8,24},{10,26},{12,28},{14,30},{16,0},... | collective-permute-start | bytes 393224 | tf_op jit(solution)/shard_map/ppermute | solution.py:172
  12.3 21.0 %collective-permute-start = (bf16[32,2048]{1,0:T(8,128)(2,1)}, bf16[32,2048]{1,0:T(8,128)(2,1)S(1)}, u32[]{:S(2)}, u32[]{:S(2)}) collective-permute-start(bf16[32,2048]{1,0:T(8,128)(2,1)} %amplitudes.1), channel_id=1, source_target_pairs={{0,8},{2,10},{4,12},{6,14},{8,0},{10,2},{12,4},{14,6},{16,24},{18,... | collective-permute-start | bytes 393224 | tf_op jit(solution)/shard_map/ppermute | solution.py:172
  19.6 13.7 %collective-permute-start.2 = (bf16[32,2048]{1,0:T(8,128)(2,1)S(1)}, bf16[32,2048]{1,0:T(8,128)(2,1)S(1)}, u32[]{:S(2)}, u32[]{:S(2)}) collective-permute-start(bf16[32,2048]{1,0:T(8,128)(2,1)S(1)} %collective-permute-done.1.refs_0_), channel_id=1, source_target_pairs={{0,8},{2,10},{4,12},{6,14},{8,0},{10,2},{12,4},{14,6},{16,24},{18,... | collective-permute-start | bytes 393224 | tf_op jit(solution)/shard_map/ppermute | solution.py:172
  20.3 0.9 %copy-start.1 = (bf16[64,2048]{1,0:T(8,128)(2,1)S(1)}, bf16[64,2048]{1,0:T(8,128)(2,1)}, u32[]{:S(2)}) copy-start(bf16[64,2048]{1,0:T(8,128)(2,1)} %left.1) | copy-start | bytes 786436
  21.3 0.9 %copy-start.2 = (bf16[32,2048]{1,0:T(8,128)(2,1)S(1)}, bf16[32,2048]{1,0:T(8,128)(2,1)}, u32[]{:S(2)}) copy-start(bf16[32,2048]{1,0:T(8,128)(2,1)} %amplitudes.1) | copy-start | bytes 393220
  22.2 16.6 %copy-start.5 = (s32[8,32]{1,0:T(8,128)S(1)}, s32[8,32]{1,0:T(8,128)}, u32[]{:S(2)}) copy-start(s32[8,32]{1,0:T(8,128)} %param.9) | copy-start | bytes 3076
  22.8 30.8 %copy-start.3 = (f32[1024]{0:T(1024)S(1)}, f32[1024]{0:T(1024)}, u32[]{:S(2)}) copy-start(f32[1024]{0:T(1024)} %param.11) | copy-start | bytes 12292
  22.8 30.8 %copy-start.4 = (f32[256]{0:T(256)S(1)}, f32[256]{0:T(256)}, u32[]{:S(2)}) copy-start(f32[256]{0:T(256)} %param.10) | copy-start | bytes 3076
  22.8 6.7 %collective-permute-start.19 = (bf16[4,32,256]{2,1,0:T(8,128)(2,1)S(1)}, bf16[4,32,256]{2,1,0:T(8,128)(2,1)S(1)}, u32[]{:S(2)}, u32[]{:S(2)}) collective-permute-start(bf16[4,32,256]{2,1,0:T(8,128)(2,1)S(1)} %get-tuple-element.33), channel_id=1, source_target_pairs={{0,16},{1,17},{2,18},{3,19},{4,20},{5,21},{6,22},{7,23},{8,24},{9,... | collective-permute-start | bytes 196616 | tf_op jit(solution)/shard_map/ppermute | solution.py:180
  26.2 7.1 %collective-permute-start.20 = (bf16[4,32,256]{2,1,0:T(8,128)(2,1)S(1)}, bf16[4,32,256]{2,1,0:T(8,128)(2,1)S(1)}, u32[]{:S(2)}, u32[]{:S(2)}) collective-permute-start(bf16[4,32,256]{2,1,0:T(8,128)(2,1)S(1)} %get-tuple-element.34), channel_id=1, source_target_pairs={{0,17},{1,16},{2,19},{3,18},{4,21},{5,20},{6,23},{7,22},{8,25},{9,... | collective-permute-start | bytes 196616 | tf_op jit(solution)/shard_map/ppermute | solution.py:180
  27.2 11.1 %collective-permute-start.16 = (f32[4,32,256]{2,1,0:T(8,128)S(1)}, f32[4,32,256]{2,1,0:T(8,128)S(1)}, u32[]{:S(2)}, u32[]{:S(2)}) collective-permute-start(f32[4,32,256]{2,1,0:T(8,128)S(1)} %get-tuple-element.32), channel_id=1, source_target_pairs={{0,1},{1,0},{2,3},{3,2},{4,5},{5,4},{6,7},{7,6},{8,9},{9,8},{10,11... | collective-permute-start | bytes 393224 | tf_op jit(solution)/shard_map/ppermute | solution.py:172
  29.5 7.5 %collective-permute-start.21 = (bf16[4,32,256]{2,1,0:T(8,128)(2,1)S(1)}, bf16[4,32,256]{2,1,0:T(8,128)(2,1)S(1)}, u32[]{:S(2)}, u32[]{:S(2)}) collective-permute-start(bf16[4,32,256]{2,1,0:T(8,128)(2,1)S(1)} %collective-permute-done.19.refs_4_), channel_id=1, source_target_pairs={{0,2},{2,0},{4,6},{6,4},{8,10},{10,8},{12,14},{14,12},{16,18},{18,... | collective-permute-start | bytes 196616 | tf_op jit(solution)/shard_map/ppermute | solution.py:172
  33.3 5.0 %collective-permute-start.22 = (bf16[4,32,256]{2,1,0:T(8,128)(2,1)S(1)}, bf16[4,32,256]{2,1,0:T(8,128)(2,1)S(1)}, u32[]{:S(2)}, u32[]{:S(2)}) collective-permute-start(bf16[4,32,256]{2,1,0:T(8,128)(2,1)S(1)} %collective-permute-done.20.refs_5_), channel_id=1, source_target_pairs={{0,2},{2,0},{4,6},{6,4},{8,10},{10,8},{12,14},{14,12},{16,18},{18,... | collective-permute-start | bytes 196616 | tf_op jit(solution)/shard_map/ppermute | solution.py:172
  33.4 23.5 %copy-start = (bf16[1024,1024]{1,0:T(8,128)(2,1)S(1)}, bf16[1024,1024]{1,0:T(8,128)(2,1)}, u32[]{:S(2)}) copy-start(bf16[1024,1024]{1,0:T(8,128)(2,1)} %refs_4_.3) | copy-start | bytes 6291460
  33.8 12.6 %collective-permute-start.9 = (bf16[4,32,256]{2,1,0:T(8,128)(2,1)S(1)}, bf16[4,32,256]{2,1,0:T(8,128)(2,1)S(1)}, u32[]{:S(2)}, u32[]{:S(2)}) collective-permute-start(bf16[4,32,256]{2,1,0:T(8,128)(2,1)S(1)} %get-tuple-element.25), channel_id=1, source_target_pairs={{0,16},{1,17},{2,18},{3,19},{4,20},{5,21},{6,22},{7,23},{8,24},{9,... | collective-permute-start | bytes 196616 | tf_op jit(solution)/shard_map/ppermute | solution.py:180
  34.0 12.5 %collective-permute-start.10 = (bf16[4,32,256]{2,1,0:T(8,128)(2,1)S(1)}, bf16[4,32,256]{2,1,0:T(8,128)(2,1)S(1)}, u32[]{:S(2)}, u32[]{:S(2)}) collective-permute-start(bf16[4,32,256]{2,1,0:T(8,128)(2,1)S(1)} %get-tuple-element.26), channel_id=1, source_target_pairs={{0,17},{1,16},{2,19},{3,18},{4,21},{5,20},{6,23},{7,22},{8,25},{9,... | collective-permute-start | bytes 196616 | tf_op jit(solution)/shard_map/ppermute | solution.py:180
  37.0 6.7 %collective-permute-start.6 = (f32[4,32,256]{2,1,0:T(8,128)S(1)}, f32[4,32,256]{2,1,0:T(8,128)S(1)}, u32[]{:S(2)}, u32[]{:S(2)}) collective-permute-start(f32[4,32,256]{2,1,0:T(8,128)S(1)} %get-tuple-element.24), channel_id=1, source_target_pairs={{0,1},{1,0},{2,3},{3,2},{4,5},{5,4},{6,7},{7,6},{8,9},{9,8},{10,11... | collective-permute-start | bytes 393224 | tf_op jit(solution)/shard_map/ppermute | solution.py:172
  38.3 5.5 %collective-permute-start.17 = (f32[4,32,256]{2,1,0:T(8,128)S(1)}, f32[4,32,256]{2,1,0:T(8,128)S(1)}, u32[]{:S(2)}, u32[]{:S(2)}) collective-permute-start(f32[4,32,256]{2,1,0:T(8,128)S(1)} %get-tuple-element.31.refs_0_), channel_id=1, source_target_pairs={{0,2},{2,0},{4,6},{6,4},{8,10},{10,8},{12,14},{14,12},{16,18},{18,... | collective-permute-start | bytes 393224 | tf_op jit(solution)/shard_map/ppermute | solution.py:172
  38.3 6.2 %collective-permute-start.18 = (f32[4,32,256]{2,1,0:T(8,128)S(1)}, f32[4,32,256]{2,1,0:T(8,128)S(1)}, u32[]{:S(2)}, u32[]{:S(2)}) collective-permute-start(f32[4,32,256]{2,1,0:T(8,128)S(1)} %collective-permute-done.16.refs_1_), channel_id=1, source_target_pairs={{0,2},{2,0},{4,6},{6,4},{8,10},{10,8},{12,14},{14,12},{16,18},{18,... | collective-permute-start | bytes 393224 | tf_op jit(solution)/shard_map/ppermute | solution.py:172
  43.8 5.9 %collective-permute-start.7 = (f32[4,32,256]{2,1,0:T(8,128)S(1)}, f32[4,32,256]{2,1,0:T(8,128)S(1)}, u32[]{:S(2)}, u32[]{:S(2)}) collective-permute-start(f32[4,32,256]{2,1,0:T(8,128)S(1)} %get-tuple-element.23.refs_0_), channel_id=1, source_target_pairs={{0,2},{2,0},{4,6},{6,4},{8,10},{10,8},{12,14},{14,12},{16,18},{18,... | collective-permute-start | bytes 393224 | tf_op jit(solution)/shard_map/ppermute | solution.py:172
  43.8 5.9 %collective-permute-start.8 = (f32[4,32,256]{2,1,0:T(8,128)S(1)}, f32[4,32,256]{2,1,0:T(8,128)S(1)}, u32[]{:S(2)}, u32[]{:S(2)}) collective-permute-start(f32[4,32,256]{2,1,0:T(8,128)S(1)} %collective-permute-done.6.refs_1_), channel_id=1, source_target_pairs={{0,2},{2,0},{4,6},{6,4},{8,10},{10,8},{12,14},{14,12},{16,18},{18,... | collective-permute-start | bytes 393224 | tf_op jit(solution)/shard_map/ppermute | solution.py:172
  44.9 7.2 %collective-permute-start.23 = (bf16[2,2,64,256]{3,2,1,0:T(8,128)(2,1)S(1)}, bf16[2,2,64,256]{3,2,1,0:T(8,128)(2,1)S(1)}, u32[]{:S(2)}, u32[]{:S(2)}) collective-permute-start(bf16[2,2,64,256]{3,2,1,0:T(8,128)(2,1)S(1)} %get-tuple-element.36), channel_id=1, source_target_pairs={{0,4},{2,6},{4,0},{6,2},{8,12},{10,14},{12,8},{14,10},{16,20},{18,... | collective-permute-start | bytes 393224 | tf_op jit(solution)/shard_map/ppermute | solution.py:172
  46.5 1.3 %collective-permute-start.11 = (bf16[4,32,256]{2,1,0:T(8,128)(2,1)S(1)}, bf16[4,32,256]{2,1,0:T(8,128)(2,1)S(1)}, u32[]{:S(2)}, u32[]{:S(2)}) collective-permute-start(bf16[4,32,256]{2,1,0:T(8,128)(2,1)S(1)} %collective-permute-done.9.refs_4_), channel_id=1, source_target_pairs={{0,2},{2,0},{4,6},{6,4},{8,10},{10,8},{12,14},{14,12},{16,18},{18,... | collective-permute-start | bytes 196616 | tf_op jit(solution)/shard_map/ppermute | solution.py:172
  46.5 1.6 %collective-permute-start.12 = (bf16[4,32,256]{2,1,0:T(8,128)(2,1)S(1)}, bf16[4,32,256]{2,1,0:T(8,128)(2,1)S(1)}, u32[]{:S(2)}, u32[]{:S(2)}) collective-permute-start(bf16[4,32,256]{2,1,0:T(8,128)(2,1)S(1)} %collective-permute-done.10.refs_5_), channel_id=1, source_target_pairs={{0,2},{2,0},{4,6},{6,4},{8,10},{10,8},{12,14},{14,12},{16,18},{18,... | collective-permute-start | bytes 196616 | tf_op jit(solution)/shard_map/ppermute | solution.py:172
  47.7 6.4 %collective-permute-start.24 = (bf16[2,2,64,256]{3,2,1,0:T(8,128)(2,1)S(1)}, bf16[2,2,64,256]{3,2,1,0:T(8,128)(2,1)S(1)}, u32[]{:S(2)}, u32[]{:S(2)}) collective-permute-start(bf16[2,2,64,256]{3,2,1,0:T(8,128)(2,1)S(1)} %get-tuple-element.37), channel_id=1, source_target_pairs={{0,8},{2,10},{4,12},{6,14},{8,0},{10,2},{12,4},{14,6},{16,24},{18,... | collective-permute-start | bytes 393224 | tf_op jit(solution)/shard_map/ppermute | solution.py:172
  48.1 8.8 %collective-permute-start.25 = (bf16[2,2,64,256]{3,2,1,0:T(8,128)(2,1)S(1)}, bf16[2,2,64,256]{3,2,1,0:T(8,128)(2,1)S(1)}, u32[]{:S(2)}, u32[]{:S(2)}) collective-permute-start(bf16[2,2,64,256]{3,2,1,0:T(8,128)(2,1)S(1)} %get-tuple-element.38), channel_id=1, source_target_pairs={{0,12},{2,14},{4,8},{6,10},{8,4},{10,6},{12,0},{14,2},{16,28},{18,... | collective-permute-start | bytes 393224 | tf_op jit(solution)/shard_map/ppermute | solution.py:172
  50.1 7.9 %collective-permute-start.13 = (bf16[2,2,64,256]{3,2,1,0:T(8,128)(2,1)S(1)}, bf16[2,2,64,256]{3,2,1,0:T(8,128)(2,1)S(1)}, u32[]{:S(2)}, u32[]{:S(2)}) collective-permute-start(bf16[2,2,64,256]{3,2,1,0:T(8,128)(2,1)S(1)} %get-tuple-element.28), channel_id=1, source_target_pairs={{0,4},{2,6},{4,0},{6,2},{8,12},{10,14},{12,8},{14,10},{16,20},{18,... | collective-permute-start | bytes 393224 | tf_op jit(solution)/shard_map/ppermute | solution.py:172
  51.7 8.1 %collective-permute-start.14 = (bf16[2,2,64,256]{3,2,1,0:T(8,128)(2,1)S(1)}, bf16[2,2,64,256]{3,2,1,0:T(8,128)(2,1)S(1)}, u32[]{:S(2)}, u32[]{:S(2)}) collective-permute-start(bf16[2,2,64,256]{3,2,1,0:T(8,128)(2,1)S(1)} %get-tuple-element.29), channel_id=1, source_target_pairs={{0,8},{2,10},{4,12},{6,14},{8,0},{10,2},{12,4},{14,6},{16,24},{18,... | collective-permute-start | bytes 393224 | tf_op jit(solution)/shard_map/ppermute | solution.py:172
  52.0 9.7 %collective-permute-start.15 = (bf16[2,2,64,256]{3,2,1,0:T(8,128)(2,1)S(1)}, bf16[2,2,64,256]{3,2,1,0:T(8,128)(2,1)S(1)}, u32[]{:S(2)}, u32[]{:S(2)}) collective-permute-start(bf16[2,2,64,256]{3,2,1,0:T(8,128)(2,1)S(1)} %get-tuple-element.30), channel_id=1, source_target_pairs={{0,12},{2,14},{4,8},{6,10},{8,4},{10,6},{12,0},{14,2},{16,28},{18,... | collective-permute-start | bytes 393224 | tf_op jit(solution)/shard_map/ppermute | solution.py:172
